TPU v7x, 32 devices: a whole 2x2x4 slice. The times are simulated.
32 devices in a mesh: segment: 4 (over z), seq: 8 (over y, x, core).
Axes of the slice: x: 2, y: 2, z: 4, core: 2. Of those that a mesh axis runs over, the one named last changes fastest.
Arguments:
- sequence: bfloat16 [256, 512, 256], P('seq', 'segment'), may hold values from -6 to 6
- first_factors: bfloat16 [4, 4, 256, 256], P('segment'), may hold values from -0.375 to 0.375
- second_factors: bfloat16 [4, 4, 256, 256], P('segment'), may hold values from -0.375 to 0.375
- kernels: bfloat16 [4, 2, 256, 256], P('segment', None, 'seq'), may hold values from -6 to 6
- gate_scale: float32 [4, 512], P('segment'), may hold values from -2 to 2
- gate_bias: float32 [4, 512], P('segment'), may hold values from -1 to 1
Outputs:
- mixed: bfloat16 [256, 512, 256], P('seq', 'segment')
All inputs are finite; a program needn't handle non-finite values.
Results may differ from a plain program's by a relative error of at most 0.024.
Values may be sent and summed in bfloat16 or wider, within the bound.
A program may use at most 64 MiB of HBM per device.

v0:
```python
import functools

import jax
import jax.numpy as jnp
from jax import lax
from jax.experimental import pallas as pl
from jax.experimental.pallas import tpu as pltpu
from jax.sharding import PartitionSpec as P

F32, BF16 = jnp.float32, jnp.bfloat16
NT = (((1,), (1,)), ((), ()))
NN = (((1,), (0,)), ((), ()))


def dot(a, b, dims):
    return lax.dot_general(a, b, dims, preferred_element_type=F32)


def kernel(
    n, nz, group, seq_in, f_own, g_own, k_own, scale_own, bias_own, out,
    raw, x_in, x, w, kk, scales, biases, kt, gv,
    own_sem, raw_sem, in_send, in_recv, out_send, out_recv, out_own,
    up_send, down_send, z_recv, sib_send, sib_recv,
    kz_send, kz_recv, gz_send, gz_recv, bz_send, bz_recv, ks_send, ks_recv, kf_send, kf_recv,
):
    s, z = lax.axis_index("seq"), lax.axis_index("segment")
    core = lax.rem(s, 2)
    sib = s + 1 - 2 * core
    channels, _, rows, radix = x.shape
    groups = channels // group
    maps = w.shape[2]
    layers = w.shape[1]
    half = n // 2

    def peer(d):
        return lax.rem(s + d, n)

    def remote(src, dst, send, recv, **where):
        return pltpu.make_async_remote_copy(
            src_ref=src, dst_ref=dst, send_sem=send, recv_sem=recv,
            device_id=where, device_id_type=pl.DeviceIdType.MESH,
        )

    def in_copy(g, d):
        t = peer(d)
        here = pl.ds(g * group, group)
        return remote(
            x_in.at[t, here], x.at[here, s], in_send.at[g, d], in_recv.at[g, d], seq=t
        )

    def out_copy(g, d):
        t = peer(d)
        here = pl.ds(g * group, group)
        return remote(
            x.at[here, t], out.at[s, here], out_send.at[g, d], out_recv.at[g, d], seq=t
        )

    def z_copy(l, i, up):
        v = w.at[core, l, i]
        sem = up_send if up else down_send
        return remote(v, v, sem.at[l, i], z_recv.at[l, i], segment=z + 1 if up else z - 1)

    def sib_copy(l, r):
        v = w.at[core, l, r]
        return remote(v, v, sib_send.at[l, r], sib_recv.at[l, r], seq=sib)

    def sib_wait(l, r):
        v = w.at[1 - core, l, r]
        remote(v, v, sib_send.at[l, r], sib_recv.at[l, r], seq=sib).wait_recv()

    def kz_copy(d, l):
        to = lax.rem(z + d, nz)
        return (
            remote(kk.at[s, l], kk.at[s, l], kz_send.at[d], kz_recv.at[d], segment=to),
            remote(scales.at[l], scales.at[l], gz_send.at[d], gz_recv.at[d], segment=to),
            remote(biases.at[l], biases.at[l], bz_send.at[d], bz_recv.at[d], segment=to),
        )

    def ks_copy(d, owner):
        v = kk.at[owner]
        return remote(v, v, ks_send.at[d], ks_recv.at[d], seq=lax.rem(s + 2 * d, n))

    def kf_copy(d, owner):
        v = kk.at[owner]
        return remote(v, v, kf_send.at[d], kf_recv.at[d], seq=sib)

    def in_wait(g, d):
        here = pl.ds(g * group, group)
        v = x.at[here, lax.rem(s + n - d, n)]
        remote(v, v, in_send.at[g, d], in_recv.at[g, d], seq=peer(d)).wait_recv()

    def out_wait(g, d):
        here = pl.ds(g * group, group)
        v = out.at[lax.rem(s + n - d, n), here]
        remote(v, v, out_send.at[g, d], out_recv.at[g, d], seq=peer(d)).wait_recv()

    own = [
        pltpu.make_async_copy(f_own.at[0], w.at[0, z], own_sem.at[0]),
        pltpu.make_async_copy(g_own.at[0], w.at[1, z], own_sem.at[1]),
        pltpu.make_async_copy(k_own.at[0], kk.at[s, z], own_sem.at[2]),
        pltpu.make_async_copy(scale_own, scales.at[z], own_sem.at[3]),
        pltpu.make_async_copy(bias_own, biases.at[z], own_sem.at[4]),
    ]
    def raw_copy(d):
        t = peer(d)
        return pltpu.make_async_copy(seq_in.at[:, t], raw.at[t], raw_sem.at[d])

    for c in own:
        c.start()
    for d in range(1, n + 1):
        raw_copy(d % n).start()

    barrier = pltpu.get_barrier_semaphore()
    mesh_id = pl.DeviceIdType.MESH

    def greet(d, _):
        pl.semaphore_signal(barrier, inc=1, device_id={"seq": peer(d)}, device_id_type=mesh_id)
        return 0

    lax.fori_loop(1, n, greet, 0)

    def greet_z(d, _):
        to = lax.rem(z + d, nz)
        pl.semaphore_signal(barrier, inc=1, device_id={"segment": to}, device_id_type=mesh_id)
        return 0

    lax.fori_loop(1, nz, greet_z, 0)
    pl.semaphore_wait(barrier, n + nz - 2)

    for c in own:
        c.wait()

    for d in range(1, nz):
        for c in kz_copy(d, z):
            c.start()

    def send_in(g, _):
        def one(d, _):
            in_copy(g, d).start()
            return 0

        return lax.fori_loop(1, n, one, 0)

    def turned(d):
        raw_copy(d).wait()
        v = raw[peer(d)]
        return jnp.swapaxes(v, 0, 1)

    def turn(d, _):
        x_in[peer(d)] = turned(d)

        @pl.when(d > 1)
        def _():
            in_copy(0, d - 1).start()

        return 0

    def send_own(up):
        for i in range(maps):
            z_copy(z, i, up).start()

    @pl.when(jnp.logical_and(z != 1, z < nz - 1))
    def _():
        send_own(True)

    @pl.when(z > 0)
    def _():
        send_own(False)

    lax.fori_loop(1, n, turn, 0)
    x[:, pl.ds(s, 1)] = turned(0)[:, None]
    in_copy(0, n - 1).start()

    for d in range(1, nz):
        for c in kz_copy(d, lax.rem(z + nz - d, nz)):
            c.wait_recv()
    for d in range(1, half):
        ks_copy(d, s).start()
    kf_copy(0, s).start()
    lax.fori_loop(1, groups, send_in, 0)

    def relay(l, i, up):
        c = z_copy(l, i, up)
        c.wait_recv()

        @pl.when((z < nz - 1) if up else (z > 0))
        def _():
            c.start()

        sib_copy(l, i).start()

    def rise(k, i):
        @pl.when(z > k)
        def _():
            relay(k, i, True)

    def fall(k, i):
        @pl.when(z + k + 1 < nz)
        def _():
            relay(z + k + 1, i, False)

    def stage(k, i):
        rise(k, i)
        fall(k, i)

    def sib_arrive(l):
        @pl.when(z != l)
        def _():
            for r in range(maps):
                sib_wait(l, r)

    for i in range(maps):
        stage(0, i)

    @pl.when(jnp.logical_and(z == 1, z < nz - 1))
    def _():
        send_own(True)

    def load(c):
        v = x[c]
        if rows % 16:
            v = v.astype(F32)
        return v.reshape(radix, radix).astype(BF16)

    def store(c, v):
        x[c] = v.reshape(n, rows, radix).astype(BF16)

    total = scales.shape[2]
    first_channel = (z * n + s) * channels

    def prepare(l, _):
        for i in range(2):
            full = kk[:, l, i].astype(F32).reshape(radix, radix)
            kt[l, i] = full.T
        pick = lax.broadcasted_iota(jnp.int32, (channels, total), 1) == (
            lax.broadcasted_iota(jnp.int32, (channels, total), 0) + first_channel
        )
        for i, values in enumerate((scales[l], biases[l])):
            col = jnp.sum(jnp.where(pick, values, 0.0), axis=1, keepdims=True)
            wide = jnp.broadcast_to(0.5 * col, (channels, radix))
            gv[l, i] = wide.reshape(channels, 1, radix)
        return 0

    def compute(l, g):
        ids = [g * group + i for i in range(group)]
        f = [w[0, l, r] for r in range(maps)]
        h = [w[1, l, r] for r in range(maps)]
        u = [load(c) for c in ids]
        y = [dot(v, f[0], NT).astype(BF16) for v in u]
        y = [(dot(h[0], v, NN) * kt[l, 0]).astype(BF16) for v in y]
        y = [dot(f[1], v, NN).astype(BF16) for v in y]
        gate = [0.5 + 0.5 * jnp.tanh(gv[l, 0, c] * v.astype(F32) + gv[l, 1, c]) for c, v in zip(ids, u)]
        y = [(dot(v, h[1], NT) * q).astype(BF16) for v, q in zip(y, gate)]
        y = [dot(v, f[2], NT).astype(BF16) for v in y]
        y = [(dot(h[2], v, NN) * kt[l, 1]).astype(BF16) for v in y]
        y = [dot(f[3], v, NN).astype(BF16) for v in y]
        for c, v, base in zip(ids, y, u):
            store(c, base.astype(F32) + dot(v, h[3], NT))

    for d in range(1, half):
        ks_copy(d, lax.rem(s + n - 2 * d, n)).wait_recv()
        kf_copy(d, lax.rem(s + n - 2 * d, n)).start()
    for d in range(half):
        kf_copy(d, lax.rem(sib + n - 2 * d, n)).wait_recv()
    lax.fori_loop(0, layers, prepare, 0)

    def step(l, g):
        @pl.when(l == 0)
        def _():
            def arrive(d, _):
                in_wait(g, d)
                return 0

            lax.fori_loop(1, n, arrive, 0)

        compute(l, g)

        @pl.when(l == layers - 1)
        def _():
            def leave(d, _):
                out_copy(g, d).start()
                return 0

            lax.fori_loop(1, n, leave, 0)
            here = pl.ds(g * group, group)
            pltpu.make_async_copy(x.at[here, s], out.at[s, here], out_own.at[g]).start()

    per = maps // groups if maps % groups == 0 else maps
    whole = max(layers - 3, 1)

    passes_on = jnp.logical_and(z > 0, z < nz - 1)

    def layer(l, _):
        @pl.when(jnp.logical_and(l + 1 < nz - 1, passes_on))
        def _():
            for i in range(maps):
                stage(l + 1, i)

        sib_arrive(l)

        def one(g, _):
            step(l, g)

            @pl.when(
                jnp.logical_and(
                    jnp.logical_and(l + 1 < nz - 1, g * per < maps), jnp.logical_not(passes_on)
                )
            )
            def _():
                for j in range(per):
                    stage(l + 1, g * per + j)

            return 0

        lax.fori_loop(0, groups, one, 0)

        return 0

    lax.fori_loop(0, whole, layer, 0)

    def last(g, _):
        def one(l, _):
            @pl.when(jnp.logical_and(g == 0, jnp.logical_and(l > whole, l < nz - 1)))
            def _():
                for i in range(maps):
                    rise(l, i)

            @pl.when(jnp.logical_and(g == 0, jnp.logical_and(l > whole + 1, l < nz)))
            def _():
                for i in range(maps):
                    fall(l - 1, i)

            @pl.when(g == 0)
            def _():
                sib_arrive(l)

            step(l, g)
            return 0

        return lax.fori_loop(whole, layers, one, 0)

    lax.fori_loop(0, groups, last, 0)

    def drain_group(g, _):
        def one(d, _):
            in_copy(g, d).wait_send()
            out_copy(g, d).wait_send()
            out_wait(g, d)
            return 0

        lax.fori_loop(1, n, one, 0)
        here = pl.ds(g * group, group)
        pltpu.make_async_copy(x.at[here, s], out.at[s, here], out_own.at[g]).wait()
        return 0

    lax.fori_loop(0, groups, drain_group, 0)

    for d in range(1, nz):
        for c in kz_copy(d, z):
            c.wait_send()
    for d in range(1, half):
        ks_copy(d, s).wait_send()
    for d in range(half):
        kf_copy(d, lax.rem(s + n - 2 * d, n)).wait_send()

    def drain_layer(l, _):
        @pl.when(z != l)
        def _():
            for r in range(maps):
                sib_copy(l, r).wait_send()

        @pl.when(jnp.logical_and(l <= z, z < nz - 1))
        def _():
            for r in range(maps):
                z_copy(l, r, True).wait_send()

        @pl.when(jnp.logical_and(l >= z, z > 0))
        def _():
            for r in range(maps):
                z_copy(l, r, False).wait_send()

        return 0

    lax.fori_loop(0, layers, drain_layer, 0)


def solution(mesh):
    n, nz = mesh.shape["seq"], mesh.shape["segment"]

    def local(sequence, first, second, kernels, scale, bias):
        rows, local_channels, radix = sequence.shape
        channels = local_channels // n
        group = min(4, channels)
        groups = channels // group
        maps = first.shape[1]
        layers = nz
        total = scale.shape[1]
        x_in = sequence.reshape(rows, n, channels, radix)
        sem = pltpu.SemaphoreType.DMA
        anywhere = pl.BlockSpec(memory_space=pl.ANY)
        result = pl.pallas_call(
            functools.partial(kernel, n, nz, group),
            out_shape=jax.ShapeDtypeStruct((n, channels, rows, radix), BF16),
            in_specs=[anywhere] * 6,
            out_specs=anywhere,
            scratch_shapes=[
                pltpu.VMEM((n, rows, channels, radix), BF16),
                pltpu.VMEM((n, channels, rows, radix), BF16),
                pltpu.VMEM((channels, n, rows, radix), BF16),
                pltpu.VMEM((2, layers, maps, radix, radix), BF16),
                pltpu.VMEM((n, layers, 2, rows, radix), BF16),
                pltpu.VMEM((layers, 1, total), F32),
                pltpu.VMEM((layers, 1, total), F32),
                pltpu.VMEM((layers, 2, radix, radix), F32),
                pltpu.VMEM((layers, 2, channels, 1, radix), F32),
                sem((5,)),
                sem((n,)),
                sem((groups, n)),
                sem((groups, n)),
                sem((groups, n)),
                sem((groups, n)),
                sem((groups,)),
                sem((layers, maps)),
                sem((layers, maps)),
                sem((layers, maps)),
                sem((layers, maps)),
                sem((layers, maps)),
                sem((nz,)),
                sem((nz,)),
                sem((nz,)),
                sem((nz,)),
                sem((nz,)),
                sem((nz,)),
                sem((n // 2,)),
                sem((n // 2,)),
                sem((n // 2,)),
                sem((n // 2,)),
            ],
            compiler_params=pltpu.CompilerParams(
                collective_id=0, has_side_effects=True, vmem_limit_bytes=56 * 2**20
            ),
        )(x_in, first, second, kernels, scale, bias)
        return result.reshape(local_channels, rows, radix).transpose(1, 0, 2)

    placed = (
        P("seq", "segment", None),
        P("segment", None, None, None),
        P("segment", None, None, None),
        P("segment", None, "seq", None),
        P("segment", None),
        P("segment", None),
    )
    return jax.shard_map(
        local, mesh=mesh, in_specs=placed, out_specs=P("seq", "segment", None), check_vma=False
    )
```

profile of v0, /device:TPU:25, one launch (start us, length us, event | category | flops | bytes accessed | tf_op | source)
XLA Modules:
  0.0 78.4 jit_solution(4725350328320752532)
XLA Ops:
  0.0 74.3 %shard_map.64 = bf16[8,16,32,256]{3,2,1,0:T(8,128)(2,1)} custom-call(bf16[32,8,16,256]{3,2,1,0:T(8,128)(2,1)} %bitcast.6, bf16[1,4,256,256]{3,2,1,0:T(8,128)(2,1)} %f_own.1, bf16[1,4,256,256]{3,2,1,0:T(8,128)(2,1)} %g_own.1, bf16[1,2,32,256]{3,2,1,0:T(8,128)(2,1)} %k_own.1, f32[1,512]{1,0:T(1,128)} %scale_own.1, f32[1,512]{1,0:T(1,128)} %bias_own.1), custom_call_target="tpu_custom_call" | custom-call | tf_op jit(solution)/shard_map/pallas_call | solution.py:401
  74.3 4.1 %copy.9 = bf16[128,32,256]{2,0,1:T(8,128)(2,1)} copy(bf16[128,32,256]{2,1,0:T(8,128)(2,1)} %bitcast.5) | data formatting | bytes 4194304 | tf_op jit(solution)/shard_map/reshape | solution.py:443
where the time goes:
time: 78.5 us; the launch traced here: 78.4 us
  Pallas kernels  74.3 us (95%)
  local copies, waits for them, and re-layouts  4.08 us (5%)
    pallas_call x1, Pallas kernels, local(): pl.pallas_call(functools.partial(kernel, n, nz, group), out_shape=jax.Sha...  74.3 us
    reshape x1, local copies, waits for them, and re-layouts, local(): return result.reshape(local_channels, rows, radix).transpose(1, 0, 2)  4.08 us

commit v1 on v0

v1 whole, which is shorter than its diff:
```python
import functools

import jax
import jax.numpy as jnp
from jax import lax
from jax.experimental import pallas as pl
from jax.experimental.pallas import tpu as pltpu
from jax.sharding import PartitionSpec as P

F32, BF16 = jnp.float32, jnp.bfloat16
NT = (((1,), (1,)), ((), ()))
NN = (((1,), (0,)), ((), ()))


def dot(a, b, dims):
    return lax.dot_general(a, b, dims, preferred_element_type=F32)


def halved(l, z, split):
    return split and ((l == 0 and z > 0) or (l == 1 and z == 0))


def pieces(l, z, maps, split):
    if halved(l, z, split):
        return [(j, True) for j in range(maps // 2)]
    return [(i, False) for i in range(maps)]


def step_order(layers, groups):
    early, lead = min(2, layers), min(2, groups)
    order = [(l, g) for g in range(lead) for l in range(early)]
    order += [(l, g) for g in range(lead) for l in range(early, layers)]
    order += [(l, g) for g in range(lead, groups) for l in range(layers)]
    return order


T0, WIRE, HOP, STEP, KZ, KS, READY = 5.0, 2.85, 1.4, 1.8, 7.5, 15.5, 18.0


def line_arrivals(nz, maps, split):
    arrive = [dict() for _ in range(nz)]
    sends = [[] for _ in range(nz)]
    for up in (True, False):
        path = range(nz - 1) if up else range(nz - 1, 0, -1)
        for z in path:
            to = z + 1 if up else z - 1
            own = pieces(z, to, maps, split)
            lead = len(own) if not up or z == 0 else min(1 if z == 1 else 2, len(own))
            free, queue = T0, [(T0, z, q) for q in own[:lead]]
            below = range(z) if up else range(z + 1, nz)
            relays = sorted(
                (arrive[z][l, q], l, q) for l in below for q in pieces(l, to, maps, split)
            )
            queue += relays
            last = relays[-1][0] if relays else T0
            queue += [(last, z, q) for q in own[lead:]]
            for at, l, q in queue:
                free = max(free, at) + WIRE
                arrive[to][l, q] = free + HOP
                if l == z:
                    sends[z].append((0.0 if at == T0 else at, l, q, up))
    return arrive, sends


def schedule(nz, maps, groups, split):
    order = step_order(nz, groups)
    arrive, sends = line_arrivals(nz, maps, split)
    plans = []
    for z in range(nz):
        acts = []
        spread = 0
        for (l, q), at in sorted(arrive[z].items(), key=lambda v: v[1]):
            to = z + 1 if l < z else z - 1
            passes = 0 <= to < nz and q in pieces(l, to, maps, split)
            acts.append((at - (1.2 if passes else 0.0), 1, "line", l, q, l < z))
            if halved(l, z, split):
                acts.append((max(at + 5.0, 17.0 + 1.5 * spread), 2, "other", l, q, l < z))
                spread += 1
        for at, l, q, up in sends[z]:
            acts.append((at - 1.19 if at else 0.0, 0 if not at else 3, "own", l, q, up))
        acts.append((KZ, 4, "kz", 0, (0, False), True))
        acts.append((KS, 4, "ks", 0, (0, False), True))
        swaps = max([at for (l, _), at in arrive[z].items() if halved(l, z, split)], default=0.0)
        late = swaps > 19.0
        for g in range(1, groups):
            if late:
                at = 14.0 if g == 1 else swaps + 0.5 + 5.8 * (g - 2)
            else:
                at = 16.0 + 5.6 * (g - 1)
            acts.append((at, 5, "in", g, (0, False), True))
        acts.sort()
        before = [a for a in acts if a[0] <= READY]
        rest = [a for a in acts if a[0] > READY]
        now, slots = READY, {}
        for t, (l, g) in enumerate(order):
            x_at = 0.0 if not g else 16.0 + 5.6 * g + 2.5
            while True:
                need = [a for a in rest if a[2] in ("line", "other") and a[3] == l]
                if rest and rest[0][0] <= now + 0.3:
                    slots.setdefault(t, []).append(rest.pop(0))
                elif not need and x_at <= now:
                    break
                else:
                    now = min([a[0] for a in rest[:1]] + ([x_at] if not need else []))
            now += STEP
        slots.setdefault(len(order) - 1, [])
        slots[len(order) - 1] += rest
        plans.append((before, slots))
    return order, plans


def kernel(
    n, nz, group, seq_in, f_own, g_own, k_own, scale_own, bias_own, out,
    raw, x_in, x, w, kk, scales, biases, kt, gv,
    own_sem, raw_sem, in_send, in_recv, out_send, out_recv, out_own,
    w_send, z_recv, sib_recv, kz_send, kz_recv, ks_send, ks_recv, kf_send, kf_recv,
):
    s, z = lax.axis_index("seq"), lax.axis_index("segment")
    core = lax.rem(s, 2)
    sib = s + 1 - 2 * core
    channels, _, rows, radix = x.shape
    groups = channels // group
    maps = w.shape[2]
    layers = w.shape[1]
    half = n // 2
    split = n == 8 and maps % 2 == 0 and nz > 2
    parity = lax.rem(lax.div(s, 2) + lax.div(s, 4), 2)
    beside = (s + 2 - 4 * lax.rem(lax.div(s, 2), 2), s + 4 - 8 * lax.rem(lax.div(s, 4), 2))
    order, plans = schedule(nz, maps, groups, split)

    def peer(d):
        return lax.rem(s + d, n)

    def remote(src, dst, send, recv, **where):
        return pltpu.make_async_remote_copy(
            src_ref=src, dst_ref=dst, send_sem=send, recv_sem=recv,
            device_id=where, device_id_type=pl.DeviceIdType.MESH,
        )

    def in_copy(g, d):
        t = peer(d)
        here = pl.ds(g * group, group)
        return remote(
            x_in.at[t, here], x.at[here, s], in_send, in_recv.at[g], seq=t
        )

    def out_copy(g, d):
        t = peer(d)
        here = pl.ds(g * group, group)
        return remote(
            x.at[here, t], out.at[s, here], out_send, out_recv, seq=t
        )

    def z_copy(l, i, up):
        v = w.at[core, l, i]
        return remote(v, v, w_send, z_recv.at[l, i], segment=z + 1 if up else z - 1)

    def ex_copy(l, i, j):
        v = w.at[core, l, i]
        return remote(v, v, w_send, z_recv.at[l, i], seq=beside[j % 2])

    def sib_copy(l, r):
        v = w.at[core, l, r]
        return remote(v, v, w_send, sib_recv.at[l], seq=sib)

    def sib_wait(l):
        v = w.at[1 - core, l]
        remote(v, v, w_send, sib_recv.at[l], seq=sib).wait_recv()

    def kz_copy(d, l):
        to = lax.rem(z + d, nz)
        return tuple(
            remote(v, v, kz_send.at[i], kz_recv.at[i], segment=to)
            for i, v in enumerate((kk.at[s, l], scales.at[l], biases.at[l]))
        )

    def kz_all():
        others = pl.ds(0, nz - 1)
        return tuple(
            remote(v, v, kz_send.at[i], kz_recv.at[i], segment=lax.rem(z + 1, nz))
            for i, v in enumerate((kk.at[s, others], scales.at[others], biases.at[others]))
        )

    def ks_copy(d, owner):
        v = kk.at[owner]
        return remote(v, v, ks_send, ks_recv, seq=lax.rem(s + 2 * d, n))

    def ks_all():
        v = kk.at[pl.ds(0, half - 1)]
        return remote(v, v, ks_send, ks_recv, seq=sib)

    def kf_copy(owner):
        v = kk.at[owner]
        return remote(v, v, kf_send, kf_recv, seq=sib)

    def kf_all():
        v = kk.at[pl.ds(0, half)]
        return remote(v, v, kf_send, kf_recv, seq=sib)

    def in_wait(g):
        v = x.at[pl.ds(g * group, group), pl.ds(0, n - 1)]
        remote(v, v, in_send, in_recv.at[g], seq=sib).wait_recv()

    own = [
        pltpu.make_async_copy(f_own.at[0], w.at[0, z], own_sem.at[0]),
        pltpu.make_async_copy(g_own.at[0], w.at[1, z], own_sem.at[1]),
        pltpu.make_async_copy(k_own.at[0], kk.at[s, z], own_sem.at[2]),
        pltpu.make_async_copy(scale_own, scales.at[z], own_sem.at[3]),
        pltpu.make_async_copy(bias_own, biases.at[z], own_sem.at[4]),
    ]
    def raw_copy(d):
        t = peer(d)
        return pltpu.make_async_copy(seq_in.at[:, t], raw.at[t], raw_sem.at[d])

    for c in own:
        c.start()
    for d in range(1, n + 1):
        raw_copy(d % n).start()

    barrier = pltpu.get_barrier_semaphore()
    mesh_id = pl.DeviceIdType.MESH

    def greet(d, _):
        pl.semaphore_signal(barrier, inc=1, device_id={"seq": peer(d)}, device_id_type=mesh_id)
        return 0

    lax.fori_loop(1, n, greet, 0)

    def greet_z(d, _):
        to = lax.rem(z + d, nz)
        pl.semaphore_signal(barrier, inc=1, device_id={"segment": to}, device_id_type=mesh_id)
        return 0

    lax.fori_loop(1, nz, greet_z, 0)
    pl.semaphore_wait(barrier, n + nz - 2)

    for c in own:
        c.wait()

    for d in range(1, nz):
        for c in kz_copy(d, z):
            c.start()

    def send_in(g, _):
        def one(d, _):
            in_copy(g, d).start()
            return 0

        return lax.fori_loop(1, n, one, 0)

    def turned(d):
        raw_copy(d).wait()
        v = raw[peer(d)]
        return jnp.swapaxes(v, 0, 1)

    def turn(d, _):
        x_in[peer(d)] = turned(d)

        @pl.when(d > 1)
        def _():
            in_copy(0, d - 1).start()

        return 0

    def mine(q):
        return 2 * q[0] + parity if q[1] else q[0]

    def onward(zz, l, q, up):
        to = zz + 1 if up else zz - 1
        return 0 <= to < nz and q in pieces(l, to, maps, split)

    def act(zz, kind, l, q, up):
        if kind == "own":
            z_copy(l, mine(q), up).start()
        elif kind == "line":
            i = mine(q)
            c = z_copy(l, i, up)
            c.wait_recv()
            if onward(zz, l, q, up):
                c.start()
            if halved(l, zz, split):
                ex_copy(l, i, q[0]).start()
            sib_copy(l, i).start()
        elif kind == "other":
            i = 2 * q[0] + 1 - parity
            ex_copy(l, i, q[0]).wait_recv()
            sib_copy(l, i).start()
        elif kind == "kz":
            for c in kz_all():
                c.wait_recv()
            for d in range(1, half):
                ks_copy(d, s).start()
            kf_copy(s).start()
        elif kind == "ks":
            ks_all().wait_recv()
            for d in range(1, half):
                kf_copy(lax.rem(s + n - 2 * d, n)).start()
        elif kind == "in":
            send_in(l, 0)

    def act_all(zz, acts):
        for a in acts:
            act(zz, *a[2:])

    for zz, (before, _) in enumerate(plans):
        @pl.when(z == zz)
        def _(zz=zz, before=before):
            act_all(zz, [a for a in before if not a[0]])

    lax.fori_loop(1, n, turn, 0)
    x[:, pl.ds(s, 1)] = turned(0)[:, None]
    in_copy(0, n - 1).start()

    for zz, (before, _) in enumerate(plans):
        @pl.when(z == zz)
        def _(zz=zz, before=before):
            act_all(zz, [a for a in before if a[0]])

    def sib_arrive(l):
        @pl.when(z != l)
        def _():
            sib_wait(l)

    def load(c):
        v = x[c]
        if rows % 16:
            v = v.astype(F32)
        return v.reshape(radix, radix).astype(BF16)

    def store(c, v):
        x[c] = v.reshape(n, rows, radix).astype(BF16)

    total = scales.shape[2]
    first_channel = (z * n + s) * channels

    def prepare(l, _):
        for i in range(2):
            full = kk[:, l, i].astype(F32).reshape(radix, radix)
            kt[l, i] = full.T
        pick = lax.broadcasted_iota(jnp.int32, (channels, total), 1) == (
            lax.broadcasted_iota(jnp.int32, (channels, total), 0) + first_channel
        )
        for i, values in enumerate((scales[l], biases[l])):
            col = jnp.sum(jnp.where(pick, values, 0.0), axis=1, keepdims=True)
            wide = jnp.broadcast_to(0.5 * col, (channels, radix))
            gv[l, i] = wide.reshape(channels, 1, radix)
        return 0

    def compute(l, g):
        ids = [g * group + i for i in range(group)]
        f = [w[0, l, r] for r in range(maps)]
        h = [w[1, l, r] for r in range(maps)]
        u = [load(c) for c in ids]
        y = [dot(v, f[0], NT).astype(BF16) for v in u]
        y = [(dot(h[0], v, NN) * kt[l, 0]).astype(BF16) for v in y]
        y = [dot(f[1], v, NN).astype(BF16) for v in y]
        gate = [0.5 + 0.5 * jnp.tanh(gv[l, 0, c] * v.astype(F32) + gv[l, 1, c]) for c, v in zip(ids, u)]
        y = [(dot(v, h[1], NT) * q).astype(BF16) for v, q in zip(y, gate)]
        y = [dot(v, f[2], NT).astype(BF16) for v in y]
        y = [(dot(h[2], v, NN) * kt[l, 1]).astype(BF16) for v in y]
        y = [dot(f[3], v, NN).astype(BF16) for v in y]
        for c, v, base in zip(ids, y, u):
            store(c, base.astype(F32) + dot(v, h[3], NT))

    kf_all().wait_recv()
    lax.fori_loop(0, layers, prepare, 0)

    def step(l, g):
        @pl.when(l == 0)
        def _():
            in_wait(g)

        compute(l, g)

        @pl.when(l == layers - 1)
        def _():
            def leave(d, _):
                out_copy(g, d).start()
                return 0

            lax.fori_loop(1, n, leave, 0)
            here = pl.ds(g * group, group)
            pltpu.make_async_copy(x.at[here, s], out.at[s, here], out_own).start()

    opens = [min(t for t, (k, _) in enumerate(order) if k == l) for l in range(layers)]

    def turn_step(t, _):
        l = sum(jnp.where(t == i, v[0], 0) for i, v in enumerate(order))
        g = sum(jnp.where(t == i, v[1], 0) for i, v in enumerate(order))
        for zz, (_, slots) in enumerate(plans):
            @pl.when(z == zz)
            def _(zz=zz, slots=slots):
                for tt, acts in slots.items():
                    @pl.when(t == tt)
                    def _(acts=acts):
                        act_all(zz, acts)

        first = sum(jnp.where(t == i, 1, 0) for i in opens)

        @pl.when(first == 1)
        def _():
            sib_arrive(l)

        step(l, g)
        return 0

    lax.fori_loop(0, len(order), turn_step, 0)

    for c in kz_all():
        c.wait_send()
    ks_all().wait_send()
    kf_all().wait_send()
    v = x_in.at[pl.ds(0, n - 1)]
    remote(v, v, in_send, in_recv.at[0], seq=sib).wait_send()

    def sent(count):
        while count:
            some = max(k for k in (1, maps, maps * layers) if k <= count)
            v = w.at[0, 0, 0] if some == 1 else (w.at[0, 0] if some == maps else w.at[0])
            remote(v, v, w_send, z_recv.at[0, 0], seq=sib).wait_send()
            count -= some

    for zz, (before, slots) in enumerate(plans):
        @pl.when(z == zz)
        def _(zz=zz, acts=before + sum(slots.values(), [])):
            count = 0
            for _, _, kind, l, q, up in acts:
                count += kind in ("own", "line", "other")
                count += kind == "line" and onward(zz, l, q, up)
                count += kind == "line" and halved(l, zz, split)
            sent(count)

    v = x.at[:, pl.ds(0, n - 1)]
    remote(v, v, out_send, out_recv, seq=sib).wait_send()
    pltpu.make_async_copy(x.at[:, s], out.at[s], out_own).wait()
    v = out.at[pl.ds(0, n - 1)]
    remote(v, v, out_send, out_recv, seq=sib).wait_recv()


def solution(mesh):
    n, nz = mesh.shape["seq"], mesh.shape["segment"]

    def local(sequence, first, second, kernels, scale, bias):
        rows, local_channels, radix = sequence.shape
        channels = local_channels // n
        group = min(4, channels)
        groups = channels // group
        maps = first.shape[1]
        layers = nz
        total = scale.shape[1]
        x_in = sequence.reshape(rows, n, channels, radix)
        sem = pltpu.SemaphoreType.DMA
        anywhere = pl.BlockSpec(memory_space=pl.ANY)
        result = pl.pallas_call(
            functools.partial(kernel, n, nz, group),
            out_shape=jax.ShapeDtypeStruct((n, channels, rows, radix), BF16),
            in_specs=[anywhere] * 6,
            out_specs=anywhere,
            scratch_shapes=[
                pltpu.VMEM((n, rows, channels, radix), BF16),
                pltpu.VMEM((n, channels, rows, radix), BF16),
                pltpu.VMEM((channels, n, rows, radix), BF16),
                pltpu.VMEM((2, layers, maps, radix, radix), BF16),
                pltpu.VMEM((n, layers, 2, rows, radix), BF16),
                pltpu.VMEM((layers, 1, total), F32),
                pltpu.VMEM((layers, 1, total), F32),
                pltpu.VMEM((layers, 2, radix, radix), F32),
                pltpu.VMEM((layers, 2, channels, 1, radix), F32),
                sem((5,)),
                sem((n,)),
                sem(()),
                sem((groups,)),
                sem(()),
                sem(()),
                sem(()),
                sem(()),
                sem((layers, maps)),
                sem((layers,)),
                sem((3,)),
                sem((3,)),
                sem(()),
                sem(()),
                sem(()),
                sem(()),
            ],
            compiler_params=pltpu.CompilerParams(
                collective_id=0, has_side_effects=True, vmem_limit_bytes=56 * 2**20
            ),
        )(x_in, first, second, kernels, scale, bias)
        return result.reshape(local_channels, rows, radix).transpose(1, 0, 2)

    placed = (
        P("seq", "segment", None),
        P("segment", None, None, None),
        P("segment", None, None, None),
        P("segment", None, "seq", None),
        P("segment", None),
        P("segment", None),
    )
    return jax.shard_map(
        local, mesh=mesh, in_specs=placed, out_specs=P("seq", "segment", None), check_vma=False
    )
```

time: 78.5 us -> 74.1 us (0.944)
  Pallas kernels: 74.3 us -> 69.3 us
    pallas_call x1, Pallas kernels: 74.3 us -> 69.3 us  [local(): pl.pallas_call(functools.partial(kernel, n, nz, group), out_shape=jax.Sha...]
where the time goes in v1:
time: 74.1 us; the launch traced here: 73.4 us
  Pallas kernels  69.3 us (94%)
  local copies, waits for them, and re-layouts  4.08 us (6%)
    pallas_call x1, Pallas kernels, local(): pl.pallas_call(functools.partial(kernel, n, nz, group), out_shape=jax.Sha...  69.3 us
    reshape x1, local copies, waits for them, and re-layouts, local(): return result.reshape(local_channels, rows, radix).transpose(1, 0, 2)  4.08 us

profile of v1, /device:TPU:25, one launch (start us, length us, event | category | flops | bytes accessed | tf_op | source)
XLA Modules:
  0.0 73.4 jit_solution(7734392303689185151)
XLA Ops:
  0.0 69.3 %shard_map.64 = bf16[8,16,32,256]{3,2,1,0:T(8,128)(2,1)} custom-call(bf16[32,8,16,256]{3,2,1,0:T(8,128)(2,1)} %bitcast.6, bf16[1,4,256,256]{3,2,1,0:T(8,128)(2,1)} %f_own.1, bf16[1,4,256,256]{3,2,1,0:T(8,128)(2,1)} %g_own.1, bf16[1,2,32,256]{3,2,1,0:T(8,128)(2,1)} %k_own.1, f32[1,512]{1,0:T(1,128)} %scale_own.1, f32[1,512]{1,0:T(1,128)} %bias_own.1), custom_call_target="tpu_custom_call" | custom-call | tf_op jit(solution)/shard_map/pallas_call | solution.py:454
  69.3 4.1 %copy.9 = bf16[128,32,256]{2,0,1:T(8,128)(2,1)} copy(bf16[128,32,256]{2,1,0:T(8,128)(2,1)} %bitcast.5) | data formatting | bytes 4194304 | tf_op jit(solution)/shard_map/reshape | solution.py:490

commit v2 on v1

--- a/solution.py
+++ b/solution.py
@@ -16,25 +16,18 @@
     return lax.dot_general(a, b, dims, preferred_element_type=F32)
 
 
-def halved(l, z, split):
-    return split and ((l == 0 and z > 0) or (l == 1 and z == 0))
+T0, WIRE, HOP, STEP, KZ, KS, READY = 5.0, 2.85, 1.4, 1.8, 7.5, 15.5, 18.0
+
+
+def halved(l, z, j, split):
+    return split and not (j > 0 and (abs(l - z) == 1 or (z == 0 and l == 2)))
 
 
 def pieces(l, z, maps, split):
-    if halved(l, z, split):
-        return [(j, True) for j in range(maps // 2)]
-    return [(i, False) for i in range(maps)]
-
-
-def step_order(layers, groups):
-    early, lead = min(2, layers), min(2, groups)
-    order = [(l, g) for g in range(lead) for l in range(early)]
-    order += [(l, g) for g in range(lead) for l in range(early, layers)]
-    order += [(l, g) for g in range(lead, groups) for l in range(layers)]
-    return order
-
-
-T0, WIRE, HOP, STEP, KZ, KS, READY = 5.0, 2.85, 1.4, 1.8, 7.5, 15.5, 18.0
+    pairs = range(maps // 2)
+    if not split:
+        return [(j, own) for j in pairs for own in (True, False)]
+    return [(j, True) for j in pairs] + [(j, False) for j in pairs if not halved(l, z, j, split)]
 
 
 def line_arrivals(nz, maps, split):
@@ -48,9 +41,7 @@
             lead = len(own) if not up or z == 0 else min(1 if z == 1 else 2, len(own))
             free, queue = T0, [(T0, z, q) for q in own[:lead]]
             below = range(z) if up else range(z + 1, nz)
-            relays = sorted(
-                (arrive[z][l, q], l, q) for l in below for q in pieces(l, to, maps, split)
-            )
+            relays = sorted((arrive[z][l, q], l, q) for l in below for q in pieces(l, to, maps, split))
             queue += relays
             last = relays[-1][0] if relays else T0
             queue += [(last, z, q) for q in own[lead:]]
@@ -62,51 +53,72 @@
     return arrive, sends
 
 
-def schedule(nz, maps, groups, split):
-    order = step_order(nz, groups)
+def passes(l, q, z, nz, maps, split):
+    to = z + 1 if l < z else z - 1
+    return l != z and 0 <= to < nz and q in pieces(l, to, maps, split)
+
+
+def transfers(z, arrive, sends, nz, maps, groups, parts, split):
+    acts, spread = [], 0
+    rising = max([at for (l, q), at in arrive.items() if l < z and passes(l, q, z, nz, maps, split)], default=0.0) - 1.15
+    for (l, q), at in sorted(arrive.items(), key=lambda v: v[1]):
+        acts.append((at - (1.2 if passes(l, q, z, nz, maps, split) else 0.0), 1, "line", l, q, l < z))
+        if q[1] and halved(l, z, q[0], split):
+            acts.append((max(at + 4.5, 17.0 + 1.5 * min(spread, 2), rising), 2, "other", l, q, l < z))
+            spread += 1
+    for at, l, q, up in sends:
+        acts.append((at - 1.19 if at else 0.0, 3 if at else 0, "own", l, q, up))
+    acts.append((KZ, 4, "kz", 0, (0, True), True))
+    acts.append((KS, 4, "ks", 0, (0, True), True))
+    at = 13.5 if z == nz - 1 else 15.5
+    for g in range(1, groups):
+        if z == 0 and g == groups - 1:
+            at = max([at] + [v + 0.1 for (l, q), v in arrive.items() if q[1] and halved(l, z, q[0], split)])
+        for part in range(parts):
+            acts.append((at, 5, "in", g, (part, True), True))
+            at = max(at + 6.0 / parts, 21.0 if z == nz - 1 else 0.0)
+    return sorted(acts, key=lambda a: a[:2])
+
+
+def schedule(nz, maps, groups, parts, split):
     arrive, sends = line_arrivals(nz, maps, split)
     plans = []
     for z in range(nz):
-        acts = []
-        spread = 0
-        for (l, q), at in sorted(arrive[z].items(), key=lambda v: v[1]):
-            to = z + 1 if l < z else z - 1
-            passes = 0 <= to < nz and q in pieces(l, to, maps, split)
-            acts.append((at - (1.2 if passes else 0.0), 1, "line", l, q, l < z))
-            if halved(l, z, split):
-                acts.append((max(at + 5.0, 17.0 + 1.5 * spread), 2, "other", l, q, l < z))
-                spread += 1
-        for at, l, q, up in sends[z]:
-            acts.append((at - 1.19 if at else 0.0, 0 if not at else 3, "own", l, q, up))
-        acts.append((KZ, 4, "kz", 0, (0, False), True))
-        acts.append((KS, 4, "ks", 0, (0, False), True))
-        swaps = max([at for (l, _), at in arrive[z].items() if halved(l, z, split)], default=0.0)
-        late = swaps > 19.0
-        for g in range(1, groups):
-            if late:
-                at = 14.0 if g == 1 else swaps + 0.5 + 5.8 * (g - 2)
-            else:
-                at = 16.0 + 5.6 * (g - 1)
-            acts.append((at, 5, "in", g, (0, False), True))
-        acts.sort()
+        acts = transfers(z, arrive[z], sends[z], nz, maps, groups, parts, split)
         before = [a for a in acts if a[0] <= READY]
         rest = [a for a in acts if a[0] > READY]
-        now, slots = READY, {}
-        for t, (l, g) in enumerate(order):
-            x_at = 0.0 if not g else 16.0 + 5.6 * g + 2.5
-            while True:
-                need = [a for a in rest if a[2] in ("line", "other") and a[3] == l]
-                if rest and rest[0][0] <= now + 0.3:
-                    slots.setdefault(t, []).append(rest.pop(0))
-                elif not need and x_at <= now:
-                    break
-                else:
-                    now = min([a[0] for a in rest[:1]] + ([x_at] if not need else []))
+        now, slots, order = READY, {}, []
+        done = [0] * groups
+        x_at = [0.0] + [a[0] + 5.0 for a in acts if a[2] == "in" and a[4][0] == parts - 1]
+        opened = set()
+        while len(order) < nz * groups:
+            t = len(order)
+            while rest and rest[0][0] <= now + 0.3:
+                slots.setdefault(t, []).append(rest.pop(0))
+            held = {a[3] for a in rest if a[2] in ("line", "other")}
+            can = [g for g in range(groups) if done[g] < nz and done[g] not in held and (done[g] or x_at[g] <= now)]
+            if not can:
+                now = min([a[0] for a in rest[:1]] + [x for g, x in enumerate(x_at) if not done[g] and x > now])
+                continue
+            g = min(can, key=lambda v: (done[v] < 2 and min(done) < 2 and v > 1, v))
+            order.append((done[g], g, done[g] not in opened))
+            opened.add(done[g])
+            done[g] += 1
             now += STEP
         slots.setdefault(len(order) - 1, [])
         slots[len(order) - 1] += rest
-        plans.append((before, slots))
-    return order, plans
+        plans.append((before, slots, order))
+    return plans
+
+
+def packed(order, layers, groups):
+    base = 2 * layers * groups
+    per = 1
+    while base ** (per + 1) < 2**30:
+        per += 1
+    digits = [(l * groups + g) * 2 + int(new) for l, g, new in order]
+    chunks = [digits[i : i + per] for i in range(0, len(digits), per)]
+    return base, per, [sum(d * base**i for i, d in enumerate(c)) for c in chunks]
 
 
 def kernel(
@@ -124,9 +136,10 @@
     layers = w.shape[1]
     half = n // 2
     split = n == 8 and maps % 2 == 0 and nz > 2
-    parity = lax.rem(lax.div(s, 2) + lax.div(s, 4), 2)
+    parity = lax.rem(lax.div(s, 2) + lax.div(s, 4), 2) if split else 0
     beside = (s + 2 - 4 * lax.rem(lax.div(s, 2), 2), s + 4 - 8 * lax.rem(lax.div(s, 4), 2))
-    order, plans = schedule(nz, maps, groups, split)
+    parts = 2 if group % 2 == 0 else 1
+    plans = schedule(nz, maps, groups, parts, split)
 
     def peer(d):
         return lax.rem(s + d, n)
@@ -137,19 +150,16 @@
             device_id=where, device_id_type=pl.DeviceIdType.MESH,
         )
 
-    def in_copy(g, d):
+    def in_copy(g, d, part=0, parts=1):
         t = peer(d)
-        here = pl.ds(g * group, group)
-        return remote(
-            x_in.at[t, here], x.at[here, s], in_send, in_recv.at[g], seq=t
-        )
-
-    def out_copy(g, d):
+        size = group // parts
+        here = pl.ds(g * group + part * size, size)
+        return remote(x_in.at[t, here], x.at[here, s], in_send, in_recv.at[g], seq=t)
+
+    def out_copy(c, size, d):
         t = peer(d)
-        here = pl.ds(g * group, group)
-        return remote(
-            x.at[here, t], out.at[s, here], out_send, out_recv, seq=t
-        )
+        here = pl.ds(c, size)
+        return remote(x.at[here, t], out.at[s, here], out_send, out_recv, seq=t)
 
     def z_copy(l, i, up):
         v = w.at[core, l, i]
@@ -157,7 +167,7 @@
 
     def ex_copy(l, i, j):
         v = w.at[core, l, i]
-        return remote(v, v, w_send, z_recv.at[l, i], seq=beside[j % 2])
+        return remote(v, v, w_send, z_recv.at[l, i], seq=jnp.where(lax.rem(core + j, 2) == 0, beside[0], beside[1]))
 
     def sib_copy(l, r):
         v = w.at[core, l, r]
@@ -241,12 +251,12 @@
         for c in kz_copy(d, z):
             c.start()
 
-    def send_in(g, _):
+    def send_in(g, part):
         def one(d, _):
-            in_copy(g, d).start()
+            in_copy(g, d, part, parts).start()
             return 0
 
-        return lax.fori_loop(1, n, one, 0)
+        lax.fori_loop(1, n, one, 0)
 
     def turned(d):
         raw_copy(d).wait()
@@ -263,11 +273,7 @@
         return 0
 
     def mine(q):
-        return 2 * q[0] + parity if q[1] else q[0]
-
-    def onward(zz, l, q, up):
-        to = zz + 1 if up else zz - 1
-        return 0 <= to < nz and q in pieces(l, to, maps, split)
+        return 2 * q[0] + (parity if q[1] else 1 - parity)
 
     def act(zz, kind, l, q, up):
         if kind == "own":
@@ -276,9 +282,9 @@
             i = mine(q)
             c = z_copy(l, i, up)
             c.wait_recv()
-            if onward(zz, l, q, up):
+            if passes(l, q, zz, nz, maps, split):
                 c.start()
-            if halved(l, zz, split):
+            if q[1] and halved(l, zz, q[0], split):
                 ex_copy(l, i, q[0]).start()
             sib_copy(l, i).start()
         elif kind == "other":
@@ -296,13 +302,13 @@
             for d in range(1, half):
                 kf_copy(lax.rem(s + n - 2 * d, n)).start()
         elif kind == "in":
-            send_in(l, 0)
+            send_in(l, q[0])
 
     def act_all(zz, acts):
         for a in acts:
             act(zz, *a[2:])
 
-    for zz, (before, _) in enumerate(plans):
+    for zz, (before, _, _) in enumerate(plans):
         @pl.when(z == zz)
         def _(zz=zz, before=before):
             act_all(zz, [a for a in before if not a[0]])
@@ -311,7 +317,7 @@
     x[:, pl.ds(s, 1)] = turned(0)[:, None]
     in_copy(0, n - 1).start()
 
-    for zz, (before, _) in enumerate(plans):
+    for zz, (before, _, _) in enumerate(plans):
         @pl.when(z == zz)
         def _(zz=zz, before=before):
             act_all(zz, [a for a in before if a[0]])
@@ -346,8 +352,8 @@
             gv[l, i] = wide.reshape(channels, 1, radix)
         return 0
 
-    def compute(l, g):
-        ids = [g * group + i for i in range(group)]
+    def compute(l, c, size):
+        ids = [c + i for i in range(size)]
         f = [w[0, l, r] for r in range(maps)]
         h = [w[1, l, r] for r in range(maps)]
         u = [load(c) for c in ids]
@@ -365,29 +371,31 @@
     kf_all().wait_recv()
     lax.fori_loop(0, layers, prepare, 0)
 
-    def step(l, g):
-        @pl.when(l == 0)
+    def step(l, g, c, size, opening):
+        @pl.when(opening)
         def _():
             in_wait(g)
 
-        compute(l, g)
+        compute(l, c, size)
 
         @pl.when(l == layers - 1)
         def _():
             def leave(d, _):
-                out_copy(g, d).start()
+                out_copy(c, size, d).start()
                 return 0
 
             lax.fori_loop(1, n, leave, 0)
-            here = pl.ds(g * group, group)
+            here = pl.ds(c, size)
             pltpu.make_async_copy(x.at[here, s], out.at[s, here], out_own).start()
 
-    opens = [min(t for t, (k, _) in enumerate(order) if k == l) for l in range(layers)]
-
-    def turn_step(t, _):
-        l = sum(jnp.where(t == i, v[0], 0) for i, v in enumerate(order))
-        g = sum(jnp.where(t == i, v[1], 0) for i, v in enumerate(order))
-        for zz, (_, slots) in enumerate(plans):
+    codes = [packed(order, layers, groups) for _, _, order in plans]
+    base, per = codes[0][:2]
+    steps = layers * groups
+
+    def turn_step(t, code):
+        digit = lax.rem(code, base)
+        l, g = lax.div(digit, 2 * groups), lax.rem(lax.div(digit, 2), groups)
+        for zz, (_, slots, _) in enumerate(plans):
             @pl.when(z == zz)
             def _(zz=zz, slots=slots):
                 for tt, acts in slots.items():
@@ -395,16 +403,22 @@
                     def _(acts=acts):
                         act_all(zz, acts)
 
-        first = sum(jnp.where(t == i, 1, 0) for i in opens)
-
-        @pl.when(first == 1)
+        @pl.when(lax.rem(digit, 2) == 1)
         def _():
             sib_arrive(l)
 
-        step(l, g)
+        step(l, g, g * group, group, l == 0)
+        return lax.div(code, base)
+
+    def run(k, _):
+        code = 0
+        for zz in range(nz):
+            for kk_, value in enumerate(codes[zz][2]):
+                code += jnp.where(jnp.logical_and(z == zz, k == kk_), value, 0)
+        lax.fori_loop(k * per, jnp.minimum(k * per + per, steps), turn_step, code)
         return 0
 
-    lax.fori_loop(0, len(order), turn_step, 0)
+    lax.fori_loop(0, len(codes[0][2]), run, 0)
 
     for c in kz_all():
         c.wait_send()
@@ -420,14 +434,14 @@
             remote(v, v, w_send, z_recv.at[0, 0], seq=sib).wait_send()
             count -= some
 
-    for zz, (before, slots) in enumerate(plans):
+    for zz, (before, slots, _) in enumerate(plans):
         @pl.when(z == zz)
         def _(zz=zz, acts=before + sum(slots.values(), [])):
             count = 0
             for _, _, kind, l, q, up in acts:
                 count += kind in ("own", "line", "other")
-                count += kind == "line" and onward(zz, l, q, up)
-                count += kind == "line" and halved(l, zz, split)
+                count += kind == "line" and passes(l, q, zz, nz, maps, split)
+                count += kind == "line" and q[1] and halved(l, zz, q[0], split)
             sent(count)
 
     v = x.at[:, pl.ds(0, n - 1)]
@@ -435,6 +449,23 @@
     pltpu.make_async_copy(x.at[:, s], out.at[s], out_own).wait()
     v = out.at[pl.ds(0, n - 1)]
     remote(v, v, out_send, out_recv, seq=sib).wait_recv()
+
+
+def turn_kernel(v, out, gone, save):
+    n, width = v.shape[:2]
+
+    def put(t):
+        here = pl.ds(t * width, width)
+        return pltpu.make_async_copy(gone.at[t], out.at[:, here], save.at[t])
+
+    def one(t, _):
+        gone[t] = jnp.swapaxes(v[t], 0, 1)
+        put(t).start()
+        return 0
+
+    lax.fori_loop(0, n, one, 0)
+    for t in range(n):
+        put(t).wait()
 
 
 def solution(mesh):
@@ -453,7 +484,7 @@
         anywhere = pl.BlockSpec(memory_space=pl.ANY)
         result = pl.pallas_call(
             functools.partial(kernel, n, nz, group),
-            out_shape=jax.ShapeDtypeStruct((n, channels, rows, radix), BF16),
+            out_shape=pltpu.VMEM((n, channels, rows, radix), BF16),
             in_specs=[anywhere] * 6,
             out_specs=anywhere,
             scratch_shapes=[
@@ -487,7 +518,13 @@
                 collective_id=0, has_side_effects=True, vmem_limit_bytes=56 * 2**20
             ),
         )(x_in, first, second, kernels, scale, bias)
-        return result.reshape(local_channels, rows, radix).transpose(1, 0, 2)
+        return pl.pallas_call(
+            turn_kernel,
+            out_shape=jax.ShapeDtypeStruct((rows, local_channels, radix), BF16),
+            in_specs=[pl.BlockSpec(memory_space=pltpu.VMEM)],
+            out_specs=anywhere,
+            scratch_shapes=[pltpu.VMEM((n, rows, channels, radix), BF16), sem((n,))],
+        )(pltpu.with_memory_space_constraint(result, pltpu.VMEM))
 
     placed = (
         P("seq", "segment", None),

time: 74.1 us -> 69 us (0.931)
  local copies, waits for them, and re-layouts: 4.08 us -> 0 us
    reshape x1 -> x0, local copies, waits for them, and re-layouts: 4.08 us -> none  [local(): return result.reshape(local_channels, rows, radix).transpose(1, 0, 2)]
    pallas_call x1 -> x2, Pallas kernels: 69.3 us -> 68.8 us  [the longest x1 67.4 us: local(): pl.pallas_call(functools.partial(kernel, n, nz, group), out_shape=pltpu.V...]
where the time goes in v2:
time: 69 us; the launch traced here: 68.8 us
  Pallas kernels  68.8 us (100%)
    pallas_call x1, Pallas kernels, local(): pl.pallas_call(functools.partial(kernel, n, nz, group), out_shape=pltpu.V...  67.4 us
    pallas_call x1, Pallas kernels, local(): pl.pallas_call(turn_kernel, out_shape=jax.ShapeDtypeStruct((rows, local_c...  1.44 us

profile of v2, /device:TPU:25, one launch (start us, length us, event | category | flops | bytes accessed | tf_op | source)
XLA Modules:
  0.0 68.8 jit_solution(15796835223015790128)
XLA Ops:
  0.0 67.4 %shard_map.64.v = bf16[8,16,32,256]{3,2,1,0:T(8,128)(2,1)S(1)} custom-call(bf16[32,8,16,256]{3,2,1,0:T(8,128)(2,1)} %bitcast.1, bf16[1,4,256,256]{3,2,1,0:T(8,128)(2,1)} %f_own.1, bf16[1,4,256,256]{3,2,1,0:T(8,128)(2,1)} %g_own.1, bf16[1,2,32,256]{3,2,1,0:T(8,128)(2,1)} %k_own.1, f32[1,512]{1,0:T(1,128)} %scale_own.1, f32[1,512]{1,0:T(1,128)} %bias_own.1), custom_call_target="tpu_custom_call" | custom-call | tf_op jit(solution)/shard_map/pallas_call | solution.py:485
  67.4 1.4 %shard_map.65 = bf16[32,128,256]{2,1,0:T(8,128)(2,1)} custom-call(bf16[8,16,32,256]{3,2,1,0:T(8,128)(2,1)S(1)} %shard_map.64.v), custom_call_target="tpu_custom_call" | custom-call | tf_op jit(solution)/shard_map/pallas_call | solution.py:521

commit v3 on v2

--- a/solution.py
+++ b/solution.py
@@ -38,8 +38,8 @@
         for z in path:
             to = z + 1 if up else z - 1
             own = pieces(z, to, maps, split)
-            lead = len(own) if not up or z == 0 else min(1 if z == 1 else 2, len(own))
-            free, queue = T0, [(T0, z, q) for q in own[:lead]]
+            lead = len(own) if not up or z == 0 else 1
+            free, queue = (T0 if z or not up else T0 - 1.6), [(T0, z, q) for q in own[:lead]]
             below = range(z) if up else range(z + 1, nz)
             relays = sorted((arrive[z][l, q], l, q) for l in below for q in pieces(l, to, maps, split))
             queue += relays
@@ -64,19 +64,23 @@
     for (l, q), at in sorted(arrive.items(), key=lambda v: v[1]):
         acts.append((at - (1.2 if passes(l, q, z, nz, maps, split) else 0.0), 1, "line", l, q, l < z))
         if q[1] and halved(l, z, q[0], split):
-            acts.append((max(at + 4.5, 17.0 + 1.5 * min(spread, 2), rising), 2, "other", l, q, l < z))
+            acts.append((max(at + (3.0 if z == 0 and l == nz - 1 else 4.5), 17.0 + 1.5 * min(spread, 2), rising), 2, "other", l, q, l < z))
             spread += 1
     for at, l, q, up in sends:
         acts.append((at - 1.19 if at else 0.0, 3 if at else 0, "own", l, q, up))
-    acts.append((KZ, 4, "kz", 0, (0, True), True))
-    acts.append((KS, 4, "ks", 0, (0, True), True))
-    at = 13.5 if z == nz - 1 else 15.5
-    for g in range(1, groups):
-        if z == 0 and g == groups - 1:
-            at = max([at] + [v + 0.1 for (l, q), v in arrive.items() if q[1] and halved(l, z, q[0], split)])
-        for part in range(parts):
-            acts.append((at, 5, "in", g, (part, True), True))
-            at = max(at + 6.0 / parts, 21.0 if z == nz - 1 else 0.0)
+    acts.append((KZ if z in (0, nz - 1) else KZ + 4.0, 4, "kz", 0, (0, True), True))
+    acts.append((KS if z in (0, nz - 1) else KS + 2.4, 4, "ks", 0, (0, True), True))
+    swaps = [v for (l, q), v in arrive.items() if q[1] and halved(l, z, q[0], split)]
+    entries = [(g, part) for g in range(1, groups) for part in range(parts)]
+    if z == nz - 1:
+        first, then, gap = [13.5, 17.9], 25.3, 1.0
+    elif z == 0:
+        first, then, gap = [15.5, 18.5, 21.5, 24.5], max(swaps, default=0.0) + 0.1, 0.1
+    else:
+        first, then, gap = [15.5, 17.0], 19.5, 3.0
+    for i, (g, part) in enumerate(entries):
+        at = first[i] if i < len(first) else then + gap * (i - len(first))
+        acts.append((at, 5, "in", g, (part, True), True))
     return sorted(acts, key=lambda a: a[:2])
 
 
@@ -100,7 +104,10 @@
             if not can:
                 now = min([a[0] for a in rest[:1]] + [x for g, x in enumerate(x_at) if not done[g] and x > now])
                 continue
-            g = min(can, key=lambda v: (done[v] < 2 and min(done) < 2 and v > 1, v))
+            if z == nz - 1:
+                g = min(can, key=lambda v: (v > 1 or done[v] > 1, v))
+            else:
+                g = min(can, key=lambda v: (done[v] < 2 and min(done) < 2 and v > 1, v))
             order.append((done[g], g, done[g] not in opened))
             opened.add(done[g])
             done[g] += 1
@@ -247,9 +254,16 @@
     for c in own:
         c.wait()
 
-    for d in range(1, nz):
+    def give_k(d):
         for c in kz_copy(d, z):
             c.start()
+
+    give_k(nz - 1)
+
+    @pl.when(z > 0)
+    def _():
+        for d in range(1, nz - 1):
+            give_k(d)
 
     def send_in(g, part):
         def one(d, _):
@@ -311,7 +325,14 @@
     for zz, (before, _, _) in enumerate(plans):
         @pl.when(z == zz)
         def _(zz=zz, before=before):
-            act_all(zz, [a for a in before if not a[0]])
+            now = [a for a in before if not a[0]]
+            if zz:
+                act_all(zz, now)
+            else:
+                act_all(zz, [a for a in now if a[4][1]])
+                for d in range(nz - 2, 0, -1):
+                    give_k(d)
+                act_all(zz, [a for a in now if not a[4][1]])
 
     lax.fori_loop(1, n, turn, 0)
     x[:, pl.ds(s, 1)] = turned(0)[:, None]

time: 69 us -> 67.2 us (0.974)
  Pallas kernels: 68.8 us -> 67 us
    pallas_call x1, Pallas kernels: 67.4 us -> 65.6 us  [local(): pl.pallas_call(functools.partial(kernel, n, nz, group), out_shape=pltpu.V...]
where the time goes in v3:
time: 67.2 us; the launch traced here: 67 us
  Pallas kernels  67 us (100%)
    pallas_call x1, Pallas kernels, local(): pl.pallas_call(functools.partial(kernel, n, nz, group), out_shape=pltpu.V...  65.6 us
    pallas_call x1, Pallas kernels, local(): pl.pallas_call(turn_kernel, out_shape=jax.ShapeDtypeStruct((rows, local_c...  1.44 us

profile of v3, /device:TPU:25, one launch (start us, length us, event | category | flops | bytes accessed | tf_op | source)
XLA Modules:
  0.0 67.0 jit_solution(8407989642535980946)
XLA Ops:
  0.0 65.6 %shard_map.64.v = bf16[8,16,32,256]{3,2,1,0:T(8,128)(2,1)S(1)} custom-call(bf16[32,8,16,256]{3,2,1,0:T(8,128)(2,1)} %bitcast.1, bf16[1,4,256,256]{3,2,1,0:T(8,128)(2,1)} %f_own.1, bf16[1,4,256,256]{3,2,1,0:T(8,128)(2,1)} %g_own.1, bf16[1,2,32,256]{3,2,1,0:T(8,128)(2,1)} %k_own.1, f32[1,512]{1,0:T(1,128)} %scale_own.1, f32[1,512]{1,0:T(1,128)} %bias_own.1), custom_call_target="tpu_custom_call" | custom-call | tf_op jit(solution)/shard_map/pallas_call | solution.py:506
  65.6 1.4 %shard_map.65 = bf16[32,128,256]{2,1,0:T(8,128)(2,1)} custom-call(bf16[8,16,32,256]{3,2,1,0:T(8,128)(2,1)S(1)} %shard_map.64.v), custom_call_target="tpu_custom_call" | custom-call | tf_op jit(solution)/shard_map/pallas_call | solution.py:542

commit v4 on v3

--- a/solution.py
+++ b/solution.py
@@ -64,7 +64,7 @@
     for (l, q), at in sorted(arrive.items(), key=lambda v: v[1]):
         acts.append((at - (1.2 if passes(l, q, z, nz, maps, split) else 0.0), 1, "line", l, q, l < z))
         if q[1] and halved(l, z, q[0], split):
-            acts.append((max(at + (3.0 if z == 0 and l == nz - 1 else 4.5), 17.0 + 1.5 * min(spread, 2), rising), 2, "other", l, q, l < z))
+            acts.append((max(at + (4.5 if z or l < nz - 1 else 3.0 if q[0] < maps // 2 - 1 else 0.3), 17.0 + 1.5 * min(spread, 2), rising), 2, "other", l, q, l < z))
             spread += 1
     for at, l, q, up in sends:
         acts.append((at - 1.19 if at else 0.0, 3 if at else 0, "own", l, q, up))
@@ -112,8 +112,8 @@
             opened.add(done[g])
             done[g] += 1
             now += STEP
-        slots.setdefault(len(order) - 1, [])
-        slots[len(order) - 1] += rest
+        if rest:
+            slots.setdefault(len(order) - 1, []).extend(rest)
         plans.append((before, slots, order))
     return plans
 
@@ -363,7 +363,7 @@
     def prepare(l, _):
         for i in range(2):
             full = kk[:, l, i].astype(F32).reshape(radix, radix)
-            kt[l, i] = full.T
+            kt[l, i] = full.T * (0.5, 1.0)[i]
         pick = lax.broadcasted_iota(jnp.int32, (channels, total), 1) == (
             lax.broadcasted_iota(jnp.int32, (channels, total), 0) + first_channel
         )
@@ -377,17 +377,17 @@
         ids = [c + i for i in range(size)]
         f = [w[0, l, r] for r in range(maps)]
         h = [w[1, l, r] for r in range(maps)]
-        u = [load(c) for c in ids]
-        y = [dot(v, f[0], NT).astype(BF16) for v in u]
+        y = [dot(load(c), f[0], NT).astype(BF16) for c in ids]
         y = [(dot(h[0], v, NN) * kt[l, 0]).astype(BF16) for v in y]
         y = [dot(f[1], v, NN).astype(BF16) for v in y]
-        gate = [0.5 + 0.5 * jnp.tanh(gv[l, 0, c] * v.astype(F32) + gv[l, 1, c]) for c, v in zip(ids, u)]
-        y = [(dot(v, h[1], NT) * q).astype(BF16) for v, q in zip(y, gate)]
+        gate = [jnp.tanh(gv[l, 0, c] * load(c).astype(F32) + gv[l, 1, c]) for c in ids]
+        y = [dot(v, h[1], NT) for v in y]
+        y = [(v + v * t).astype(BF16) for v, t in zip(y, gate)]
         y = [dot(v, f[2], NT).astype(BF16) for v in y]
         y = [(dot(h[2], v, NN) * kt[l, 1]).astype(BF16) for v in y]
         y = [dot(f[3], v, NN).astype(BF16) for v in y]
-        for c, v, base in zip(ids, y, u):
-            store(c, base.astype(F32) + dot(v, h[3], NT))
+        for c, v in zip(ids, y):
+            store(c, load(c).astype(F32) + dot(v, h[3], NT))
 
     kf_all().wait_recv()
     lax.fori_loop(0, layers, prepare, 0)
@@ -412,17 +412,20 @@
     codes = [packed(order, layers, groups) for _, _, order in plans]
     base, per = codes[0][:2]
     steps = layers * groups
+    last_slot = max(t for _, slots, _ in plans for t, acts in slots.items() if acts)
 
     def turn_step(t, code):
         digit = lax.rem(code, base)
         l, g = lax.div(digit, 2 * groups), lax.rem(lax.div(digit, 2), groups)
-        for zz, (_, slots, _) in enumerate(plans):
-            @pl.when(z == zz)
-            def _(zz=zz, slots=slots):
-                for tt, acts in slots.items():
-                    @pl.when(t == tt)
-                    def _(acts=acts):
-                        act_all(zz, acts)
+        @pl.when(t <= last_slot)
+        def _():
+            for zz, (_, slots, _) in enumerate(plans):
+                @pl.when(z == zz)
+                def _(zz=zz, slots=slots):
+                    for tt, acts in slots.items():
+                        @pl.when(t == tt)
+                        def _(acts=acts):
+                            act_all(zz, acts)
 
         @pl.when(lax.rem(digit, 2) == 1)
         def _():

time: 67.2 us -> 66.9 us (level); the launches traced: 67 us -> 65.7 us
  Pallas kernels: 67 us -> 65.7 us
    pallas_call x1, Pallas kernels: 65.6 us -> 64.3 us  [local(): pl.pallas_call(functools.partial(kernel, n, nz, group), out_shape=pltpu.V...]
where the time goes in v4:
time: 66.9 us; the launch traced here: 65.7 us
  Pallas kernels  65.7 us (98%)
    pallas_call x1, Pallas kernels, local(): pl.pallas_call(functools.partial(kernel, n, nz, group), out_shape=pltpu.V...  64.3 us
    pallas_call x1, Pallas kernels, local(): pl.pallas_call(turn_kernel, out_shape=jax.ShapeDtypeStruct((rows, local_c...  1.44 us

profile of v4, /device:TPU:25, one launch (start us, length us, event | category | flops | bytes accessed | tf_op | source)
XLA Modules:
  0.0 65.7 jit_solution(14691534225364449086)
XLA Ops:
  0.0 64.3 %shard_map.64.v = bf16[8,16,32,256]{3,2,1,0:T(8,128)(2,1)S(1)} custom-call(bf16[32,8,16,256]{3,2,1,0:T(8,128)(2,1)} %bitcast.1, bf16[1,4,256,256]{3,2,1,0:T(8,128)(2,1)} %f_own.1, bf16[1,4,256,256]{3,2,1,0:T(8,128)(2,1)} %g_own.1, bf16[1,2,32,256]{3,2,1,0:T(8,128)(2,1)} %k_own.1, f32[1,512]{1,0:T(1,128)} %scale_own.1, f32[1,512]{1,0:T(1,128)} %bias_own.1), custom_call_target="tpu_custom_call" | custom-call | tf_op jit(solution)/shard_map/pallas_call | solution.py:509
  64.3 1.4 %shard_map.65 = bf16[32,128,256]{2,1,0:T(8,128)(2,1)} custom-call(bf16[8,16,32,256]{3,2,1,0:T(8,128)(2,1)S(1)} %shard_map.64.v), custom_call_target="tpu_custom_call" | custom-call | tf_op jit(solution)/shard_map/pallas_call | solution.py:545

commit v5 on v4

--- a/solution.py
+++ b/solution.py
@@ -75,7 +75,7 @@
     if z == nz - 1:
         first, then, gap = [13.5, 17.9], 25.3, 1.0
     elif z == 0:
-        first, then, gap = [15.5, 18.5, 21.5, 24.5], max(swaps, default=0.0) + 0.1, 0.1
+        first, then, gap = [15.5, 18.5, 21.5, 24.5], max(swaps, default=0.0), 0.0
     else:
         first, then, gap = [15.5, 17.0], 19.5, 3.0
     for i, (g, part) in enumerate(entries):

time: 66.9 us -> 67 us (level)
  no operation moved by 1% of the time
where the time goes in v5:
time: 67 us; the launch traced here: 65.7 us
  Pallas kernels  65.7 us (98%)
    pallas_call x1, Pallas kernels, local(): pl.pallas_call(functools.partial(kernel, n, nz, group), out_shape=pltpu.V...  64.3 us
    pallas_call x1, Pallas kernels, local(): pl.pallas_call(turn_kernel, out_shape=jax.ShapeDtypeStruct((rows, local_c...  1.44 us

profile of v5, /device:TPU:25, one launch (start us, length us, event | category | flops | bytes accessed | tf_op | source)
XLA Modules:
  0.0 65.7 jit_solution(12346865340624812324)
XLA Ops:
  0.0 64.3 %shard_map.64.v = bf16[8,16,32,256]{3,2,1,0:T(8,128)(2,1)S(1)} custom-call(bf16[32,8,16,256]{3,2,1,0:T(8,128)(2,1)} %bitcast.1, bf16[1,4,256,256]{3,2,1,0:T(8,128)(2,1)} %f_own.1, bf16[1,4,256,256]{3,2,1,0:T(8,128)(2,1)} %g_own.1, bf16[1,2,32,256]{3,2,1,0:T(8,128)(2,1)} %k_own.1, f32[1,512]{1,0:T(1,128)} %scale_own.1, f32[1,512]{1,0:T(1,128)} %bias_own.1), custom_call_target="tpu_custom_call" | custom-call | tf_op jit(solution)/shard_map/pallas_call | solution.py:509
  64.3 1.4 %shard_map.65 = bf16[32,128,256]{2,1,0:T(8,128)(2,1)} custom-call(bf16[8,16,32,256]{3,2,1,0:T(8,128)(2,1)S(1)} %shard_map.64.v), custom_call_target="tpu_custom_call" | custom-call | tf_op jit(solution)/shard_map/pallas_call | solution.py:545
